TPU v7x, 32 devices: a whole 2x2x4 slice. The times are simulated.
32 devices in a mesh: dp: 4 (over z), tensor: 8 (over y, x, core).
Axes of the slice: x: 2, y: 2, z: 4, core: 2. Of those that a mesh axis runs over, the one named last changes fastest.
Arguments:
- activations: bfloat16 [3072, 4096], P('dp', 'tensor'), may hold values from -6 to 6
- out_grads_t: bfloat16 [5504, 3072], P('tensor', 'dp'), may hold values from -6 to 6
- in_basis: bfloat16 [4096, 4096], P(None, 'tensor'), may hold values from -0.09375 to 0.09375
- out_basis_t: bfloat16 [5504, 5504], P('tensor'), may hold values from -0.078125 to 0.078125
- query_proj: bfloat16 [4, 5504, 4096], P(None, 'tensor', 'dp'), may hold values from -6 to 6
- eigvals: float32 [5504, 4096], P('tensor', 'dp'), may hold values from 0.05 to 5
- damping: float32 [1], replicated, may hold values from 0.05 to 0.2
- lengths: int32 [24], P('dp'), may hold values from 1 to 128, 1920 in all
Outputs:
- scores: float32 [24, 4], P('dp')
Inputs may be any that keep to these rules, and one draw needn't show every extreme that they name: `lengths`: the largest token count is exactly 128.
All inputs are finite; a program needn't handle non-finite values. No bound on the sum of `lengths` on one device may be relied on, other than what follows from the above.
Results may differ from a plain program's by a relative error of at most 0.006.
Values may be sent and summed in bfloat16 or wider, within the bound.
A program may use at most 128 MiB of HBM per device.

v0:
```python
import jax
import jax.numpy as jnp
from jax import lax
from jax.sharding import PartitionSpec as P


def local(activations, out_grads_t, in_basis, out_basis_t, query_proj, eigvals, damping, lengths):
    full_act = lax.all_gather(activations, "tensor", axis=1, tiled=True)
    act_local = jnp.dot(full_act, in_basis, preferred_element_type=jnp.float32).astype(jnp.bfloat16)
    act_proj = lax.all_gather(act_local, "tensor", axis=1, tiled=True)
    token_rows = full_act.shape[0]
    width = out_basis_t.shape[0]
    grad_full = jnp.dot(
        out_basis_t,
        lax.all_gather(out_grads_t, "tensor", axis=0, tiled=True),
        preferred_element_type=jnp.float32,
    )
    seq_count = lengths.shape[0]
    seq_len = token_rows // seq_count
    position = lax.broadcasted_iota(jnp.int32, (seq_count, seq_len), 1)
    keep = (position < lengths[:, None]).astype(jnp.float32).reshape(1, token_rows)
    grad_proj = (grad_full * keep).astype(jnp.bfloat16)
    scaled = (query_proj.astype(jnp.float32) / (eigvals + damping[0])).astype(jnp.bfloat16)
    query_count = query_proj.shape[0]
    mixed = jnp.einsum(
        "td,qjd->qjt",
        act_proj,
        lax.all_gather(scaled, "dp", axis=2, tiled=True),
        preferred_element_type=jnp.float32,
    )
    weighted = mixed * grad_proj.astype(jnp.float32)[None, :, :]
    partial_value = jnp.sum(weighted.reshape(query_count, width, seq_count, seq_len), axis=(1, 3)).T
    totals = lax.psum(partial_value, "tensor")
    norm_factor = (act_proj.shape[1] * out_basis_t.shape[1] * seq_len) ** (-0.5)
    return totals * norm_factor


def solution(mesh):
    placed = (
        P("dp", "tensor"),
        P("tensor", "dp"),
        P(None, "tensor"),
        P("tensor", None),
        P(None, "tensor", "dp"),
        P("tensor", "dp"),
        P(),
        P("dp"),
    )
    return jax.shard_map(
        local, mesh=mesh, in_specs=placed, out_specs=P("dp", None), check_vma=False
    )
```

profile of v0, /device:TPU:0, one launch (start us, length us, event | category | flops | bytes accessed | tf_op | source)
XLA Modules:
  0.0 591.1 jit_solution(7677577895891891836)
XLA Ops:
  6.5 0.0 all-gather.7.cloned.1.call-start
  6.5 0.7 all-gather.7.cloned.1.call-update
  7.3 0.0 all-gather.11.cloned.1.call-start
  7.3 0.7 all-gather.11.cloned.1.call-update
  8.0 0.0 copy-start
  8.0 0.0 all-gather.9.cloned.1.call-start
  8.1 50.5 %all-gather.7.cloned.1.call-done = bf16[768,4096]{1,0:T(8,128)(2,1)} async-done(((bf16[768,512]{1,0:T(8,128)(2,1)}), bf16[768,4096]{1,0:T(8,128)(2,1)}) %all-gather.7.cloned.1.call-update) | async-done | bytes 6291472 | tf_op jit(solution)/shard_map/all_gather | solution.py:8
  58.5 8.3 %convolution_convert_fusion = bf16[768,512]{1,0:T(8,128)(2,1)} fusion(bf16[768,4096]{1,0:T(8,128)(2,1)} %all-gather.7.cloned.1.call-done, bf16[4096,512]{1,0:T(8,128)(2,1)} %param.10), kind=kOutput, calls=%fused_computation.7 | convolution fusion | flops 3221618688 | bytes 11272192 | tf_op jit(solution)/shard_map/dot_general | solution.py:9
  66.9 0.0 all-gather.9.cloned.1.call-update
  66.9 0.0 all-gather.5.cloned.1.call-start
  67.6 0.0 copy-done
  67.6 0.5 broadcast_add_fusion
  68.1 0.0 copy-start.1
  68.1 7.5 %divide_convert_fusion = bf16[4,688,1024]{2,1,0:T(8,128)(2,1)} fusion(bf16[4,688,1024]{2,1,0:T(8,128)(2,1)} %param.12, f32[688,1024]{1,0:T(8,128)S(1)} %broadcast_add_fusion), kind=kLoop, calls=%fused_computation | loop fusion | flops 8454144 | bytes 14090240 | tf_op jit(solution)/shard_map/convert_element_type | solution.py:23
  75.6 0.0 all-gather.5.cloned.1.call-update
  75.6 0.0 copy-done.1
  75.6 0.1 convert_bitcast_fusion
  75.7 39.3 %all-gather.11.cloned.1.call-done = bf16[5504,768]{1,0:T(8,128)(2,1)} async-done(((bf16[688,768]{1,0:T(8,128)(2,1)}), bf16[5504,768]{1,0:T(8,128)(2,1)}) %all-gather.11.cloned.1.call-update) | async-done | bytes 8454160 | tf_op jit(solution)/shard_map/all_gather | solution.py:15
  115.0 10.9 %fusion.4 = f32[688,768]{1,0:T(8,128)S(1)} fusion(bf16[688,5504]{1,0:T(8,128)(2,1)} %param.11, bf16[5504,768]{1,0:T(8,128)(2,1)} %all-gather.11.cloned.1.call-done, f32[768]{0:T(1024)S(1)} %convert_bitcast_fusion), kind=kOutput, calls=%fused_computation.5 | convolution fusion | flops 5818036224 | bytes 18144256 | tf_op jit(solution)/shard_map/dot_general | solution.py:13
  125.9 37.6 %all-gather.9.cloned.1.call-done = bf16[768,4096]{1,0:T(8,128)(2,1)} async-done(((bf16[768,512]{1,0:T(8,128)(2,1)}), bf16[768,4096]{1,0:T(8,128)(2,1)}) %all-gather.9.cloned.1.call-update) | async-done | bytes 6291472 | tf_op jit(solution)/shard_map/all_gather | solution.py:10
  163.5 384.0 %all-gather.5.cloned.1.call-done = bf16[4,688,4096]{2,1,0:T(8,128)(2,1)} async-done(((bf16[4,688,1024]{2,1,0:T(8,128)(2,1)}), bf16[4,688,4096]{2,1,0:T(8,128)(2,1)}) %all-gather.5.cloned.1.call-update) | async-done | bytes 22544400 | tf_op jit(solution)/shard_map/all_gather | solution.py:28
  547.5 22.8 %multiply_reduce_fusion = f32[4,768]{1,0:T(4,128)S(1)} fusion(f32[688,768]{1,0:T(8,128)S(1)} %fusion.4, bf16[4,688,4096]{2,1,0:T(8,128)(2,1)} %all-gather.5.cloned.1.call-done, bf16[768,4096]{1,0:T(8,128)(2,1)} %all-gather.9.cloned.1.call-done), kind=kOutput, calls=%fused_computation.1 | convolution fusion | flops 17318309888 | bytes 30961664 | tf_op jit(solution)/shard_map/td,qjd->qjt/dot_general | solution.py:25
  570.3 0.1 reduce_sum.18
  570.4 13.6 %psum.7 = f32[6,4]{0,1:T(4,128)S(1)} all-reduce(f32[6,4]{0,1:T(4,128)S(1)} %bitcast.15), channel_id=1, replica_groups=mesh['dp'=4,'tensor'=8] {'tensor'}, use_global_device_ids=true, to_apply=%region_2.3 | all-reduce | flops 24 | bytes 192 | tf_op jit(solution)/shard_map/psum | solution.py:33
  584.0 0.6 broadcast_multiply_fusion
  (1 shorter events, 0.0 us)
Async XLA Ops:
  6.5 52.0 %all-gather.7.cloned.1.call-start = ((), (), s32[]{:S(2)}) async-start(), calls=%async_computation.1 | async-start | bytes 7077888 | tf_op jit(solution)/shard_map/all_gather | solution.py:8
  7.3 107.7 %all-gather.11.cloned.1.call-start = ((), (), s32[]{:S(2)}) async-start(), calls=%async_computation.3 | async-start | bytes 9510912 | tf_op jit(solution)/shard_map/all_gather | solution.py:15
  8.0 59.6 %copy-start = (f32[688,1024]{1,0:T(8,128)S(1)}, f32[688,1024]{1,0:T(8,128)}, u32[]{:S(2)}) copy-start(f32[688,1024]{1,0:T(8,128)} %param.13) | copy-start | bytes 8454148
  8.0 155.5 %all-gather.9.cloned.1.call-start = ((), (), s32[]{:S(2)}) async-start(), calls=%async_computation.2 | async-start | bytes 7077888 | tf_op jit(solution)/shard_map/all_gather | solution.py:10
  66.9 480.6 %all-gather.5.cloned.1.call-start = ((), (), s32[]{:S(2)}) async-start(), calls=%async_computation | async-start | bytes 28180480 | tf_op jit(solution)/shard_map/all_gather | solution.py:28
  68.1 7.5 %copy-start.1 = (s32[6]{0:T(128)S(1)}, s32[6]{0:T(128)}, u32[]{:S(2)}) copy-start(s32[6]{0:T(128)} %param.15) | copy-start | bytes 76
Sparse Core Ops, SparseCore 0:
  9.2 49.2 all-gather.6
  60.4 54.5 all-gather.10
  116.9 46.5 all-gather.8
  164.9 382.4 all-gather.4
where the time goes:
time: 591 us
  waiting for transfers between devices  513 us (87%)
  matrix products  42 us (7%)
  between operations  13.8 us (2%)
  blocking collectives  13.6 us (2%)
  other arithmetic  8.66 us (1%)
    all_gather x1, waiting for transfers between devices, local(): lax.all_gather(scaled, 'dp', axis=2, tiled=True)  384 us
    all_gather x1, waiting for transfers between devices, local(): full_act = lax.all_gather(activations, 'tensor', axis=1, tiled=True)  50.5 us
    all_gather x1, waiting for transfers between devices, local(): lax.all_gather(out_grads_t, 'tensor', axis=0, tiled=True)  39.3 us
    all_gather x1, waiting for transfers between devices, local(): act_proj = lax.all_gather(act_local, 'tensor', axis=1, tiled=True)  37.6 us
    dot_general x1, matrix products, local(): jnp.einsum('td,qjd->qjt', act_proj, lax.all_gather(scaled, 'dp', axis=2,...  22.8 us
    psum x1, blocking collectives, local(): totals = lax.psum(partial_value, 'tensor')  13.6 us
  transfers between devices with their start and end apart: 4, of which 4 were waited for; matrix products, arithmetic and copies ran while one was open for 5% of the time, Pallas kernels for 0%

commit v1 on v0

--- a/solution.py
+++ b/solution.py
@@ -22,12 +22,22 @@
     grad_proj = (grad_full * keep).astype(jnp.bfloat16)
     scaled = (query_proj.astype(jnp.float32) / (eigvals + damping[0])).astype(jnp.bfloat16)
     query_count = query_proj.shape[0]
-    mixed = jnp.einsum(
-        "td,qjd->qjt",
-        act_proj,
-        lax.all_gather(scaled, "dp", axis=2, tiled=True),
-        preferred_element_type=jnp.float32,
-    )
+    size, index, extent = (lax.axis_size("dp"), lax.axis_index("dp"), scaled.shape[2])
+    ahead = [(i, (i + 1) % size) for i in range(size)]
+    block, total = (scaled, None)
+    for lap in range(size):
+        following = lax.ppermute(block, "dp", ahead) if lap < size - 1 else None
+        absorb = jnp.einsum(
+            "td,qjd->qjt",
+            lax.dynamic_slice_in_dim(
+                act_proj, (index - lap) % size * extent, block.shape[2], axis=1
+            ),
+            block,
+            preferred_element_type=jnp.float32,
+        )
+        total = absorb if total is None else total + absorb
+        block = following
+    mixed = total
     weighted = mixed * grad_proj.astype(jnp.float32)[None, :, :]
     partial_value = jnp.sum(weighted.reshape(query_count, width, seq_count, seq_len), axis=(1, 3)).T
     totals = lax.psum(partial_value, "tensor")

time: 591 us -> 427 us (0.72)
  waiting for transfers between devices: 513 us -> 325 us
  matrix products: 42 us -> 64.8 us
    all_gather x1 -> x0, waiting for transfers between devices: 384 us -> none  [local(): lax.all_gather(scaled, 'dp', axis=2, tiled=True)]
    ppermute x0 -> x3, waiting for transfers between devices: none -> 284 us  [local(): following = lax.ppermute(block, 'dp', ahead) if lap < size - 1 else None]
    all_gather x1, waiting for transfers between devices: 39.3 us -> 0.01 us  [local(): lax.all_gather(out_grads_t, 'tensor', axis=0, tiled=True)]
    all_gather x1, waiting for transfers between devices: 37.6 us -> 0.02 us  [local(): act_proj = lax.all_gather(act_local, 'tensor', axis=1, tiled=True)]
    dot_general x1 -> x4, matrix products: 22.8 us -> 45.6 us  [local(): jnp.einsum('td,qjd->qjt', lax.dynamic_slice_in_dim(act_proj, (index - lap...]
    all_gather x1, waiting for transfers between devices: 50.5 us -> 39.5 us  [local(): full_act = lax.all_gather(activations, 'tensor', axis=1, tiled=True)]
  transfers between devices with their start and end apart: 4 -> 6, of which waited for: 4 -> 4; matrix products, arithmetic and copies ran while one was open for 5% -> 13% of each run, Pallas kernels for 0% -> 0%
where the time goes in v1:
time: 427 us
  waiting for transfers between devices  325 us (76%)
  matrix products  64.8 us (15%)
  between operations  14 us (3%)
  blocking collectives  11.8 us (3%)
  other arithmetic  7.45 us (2%)
    ppermute x3, waiting for transfers between devices, local(): following = lax.ppermute(block, 'dp', ahead) if lap < size - 1 else None  284 us
    dot_general x4, matrix products, local(): jnp.einsum('td,qjd->qjt', lax.dynamic_slice_in_dim(act_proj, (index - lap...  45.6 us
    all_gather x1, waiting for transfers between devices, local(): full_act = lax.all_gather(activations, 'tensor', axis=1, tiled=True)  39.5 us
    psum x1, blocking collectives, local(): totals = lax.psum(partial_value, 'tensor')  11.8 us
    dot_general x1, matrix products, local(): jnp.dot(out_basis_t, lax.all_gather(out_grads_t, 'tensor', axis=0, tiled=...  10.9 us
  transfers between devices with their start and end apart: 6, of which 4 were waited for; matrix products, arithmetic and copies ran while one was open for 13% of the time, Pallas kernels for 0%

profile of v1, /device:TPU:0, one launch (start us, length us, event | category | flops | bytes accessed | tf_op | source)
XLA Modules:
  0.0 426.6 jit_solution(1255649011960453041)
XLA Ops:
  6.5 0.0 all-gather.4.cloned.1.call-start
  6.5 0.7 all-gather.4.cloned.1.call-update
  7.3 0.0 all-gather.8.cloned.1.call-start
  7.3 0.7 all-gather.8.cloned.1.call-update
  8.0 0.0 all-gather.6.cloned.1.call-start
  8.1 0.0 copy-start
  8.9 2.2 broadcast_add_fusion
  11.1 0.5 copy-done
  11.5 4.5 %divide_convert_fusion = bf16[4,688,1024]{2,1,0:T(8,128)(2,1)} fusion(bf16[4,688,1024]{2,1,0:T(8,128)(2,1)S(1)} %copy-done, f32[688,1024]{1,0:T(8,128)S(1)} %broadcast_add_fusion), kind=kLoop, calls=%fused_computation | loop fusion | flops 8454144 | bytes 14090240 | tf_op jit(solution)/shard_map/convert_element_type | solution.py:23
  16.0 0.0 copy-start.1
  16.0 3.1 collective-permute-start
  19.1 39.5 %all-gather.4.cloned.1.call-done = bf16[768,4096]{1,0:T(8,128)(2,1)} async-done(((bf16[768,512]{1,0:T(8,128)(2,1)}), bf16[768,4096]{1,0:T(8,128)(2,1)}) %all-gather.4.cloned.1.call-update) | async-done | bytes 6291472 | tf_op jit(solution)/shard_map/all_gather | solution.py:8
  58.5 8.3 %convolution_convert_fusion = bf16[768,512]{1,0:T(8,128)(2,1)} fusion(bf16[768,4096]{1,0:T(8,128)(2,1)} %all-gather.4.cloned.1.call-done, bf16[4096,512]{1,0:T(8,128)(2,1)} %param.10), kind=kOutput, calls=%fused_computation.16 | convolution fusion | flops 3221618688 | bytes 11272192 | tf_op jit(solution)/shard_map/dot_general | solution.py:9
  66.8 0.0 all-gather.6.cloned.1.call-update
  66.9 76.0 %collective-permute-done = bf16[4,688,1024]{2,1,0:T(8,128)(2,1)} collective-permute-done((bf16[4,688,1024]{2,1,0:T(8,128)(2,1)}, bf16[4,688,1024]{2,1,0:T(8,128)(2,1)}, u32[]{:S(2)}, u32[]{:S(2)}) %collective-permute-start) | collective-permute-done | bytes 5636128 | tf_op jit(solution)/shard_map/ppermute | solution.py:29
  142.9 0.0 collective-permute-start.1
  142.9 124.7 %collective-permute-done.1 = bf16[4,688,1024]{2,1,0:T(8,128)(2,1)} collective-permute-done((bf16[4,688,1024]{2,1,0:T(8,128)(2,1)}, bf16[4,688,1024]{2,1,0:T(8,128)(2,1)}, u32[]{:S(2)}, u32[]{:S(2)}) %collective-permute-start.1) | collective-permute-done | bytes 5636128 | tf_op jit(solution)/shard_map/ppermute | solution.py:29
  267.6 0.0 collective-permute-start.2
  267.6 0.0 copy-done.1
  267.6 0.1 convert_bitcast_fusion
  267.7 0.0 all-gather.8.cloned.1.call-done
  267.7 10.9 %fusion.11 = f32[688,768]{1,0:T(8,128)S(1)} fusion(bf16[688,5504]{1,0:T(8,128)(2,1)} %param.11, bf16[5504,768]{1,0:T(8,128)(2,1)} %all-gather.8.cloned.1.call-done, f32[768]{0:T(1024)S(1)} %convert_bitcast_fusion), kind=kOutput, calls=%fused_computation.14 | convolution fusion | flops 5818036224 | bytes 18144256 | tf_op jit(solution)/shard_map/dot_general | solution.py:13
  278.6 0.0 all-gather.6.cloned.1.call-done
  278.7 0.0 copy-start.2
  278.7 11.1 %fusion.1 = f32[4,688,768]{2,1,0:T(8,128)} fusion(bf16[4,688,1024]{2,1,0:T(8,128)(2,1)} %collective-permute-done.1, bf16[768,4096]{1,0:T(8,128)(2,1)} %all-gather.6.cloned.1.call-done, s32[]{:T(128)S(6)} %select_n.36), kind=kOutput, calls=%fused_computation.4 | convolution fusion | flops 4328521728 | bytes 15663108 | tf_op jit(solution)/shard_map/td,qjd->qjt/dot_general | solution.py:30
  289.7 0.0 copy-done.2
  289.7 9.2 %fusion.3 = f32[4,688,768]{2,1,0:T(8,128)} fusion(bf16[4,688,1024]{2,1,0:T(8,128)(2,1)} %collective-permute-done, bf16[768,4096]{1,0:T(8,128)(2,1)S(1)} %copy-done.2, s32[]{:T(128)S(6)} %select_n.34), kind=kOutput, calls=%fused_computation.6 | convolution fusion | flops 4328521728 | bytes 15663108 | tf_op jit(solution)/shard_map/td,qjd->qjt/dot_general | solution.py:30
  298.9 9.3 %fusion.5 = f32[4,688,768]{2,1,0:T(8,128)} fusion(bf16[4,688,1024]{2,1,0:T(8,128)(2,1)} %divide_convert_fusion, bf16[768,4096]{1,0:T(8,128)(2,1)S(1)} %copy-done.2, s32[]{:T(128)S(6)} %select_n.32), kind=kOutput, calls=%fused_computation.8 | convolution fusion | flops 4328521728 | bytes 15663108 | tf_op jit(solution)/shard_map/td,qjd->qjt/dot_general | solution.py:30
  308.2 83.3 %collective-permute-done.2 = bf16[4,688,1024]{2,1,0:T(8,128)(2,1)} collective-permute-done((bf16[4,688,1024]{2,1,0:T(8,128)(2,1)}, bf16[4,688,1024]{2,1,0:T(8,128)(2,1)}, u32[]{:S(2)}, u32[]{:S(2)}) %collective-permute-start.2) | collective-permute-done | bytes 5636128 | tf_op jit(solution)/shard_map/ppermute | solution.py:29
  391.5 16.1 %multiply_reduce_fusion = f32[4,768]{1,0:T(4,128)S(1)} fusion(f32[4,688,768]{2,1,0:T(8,128)} %fusion.1, f32[4,688,768]{2,1,0:T(8,128)} %fusion.5, f32[4,688,768]{2,1,0:T(8,128)} %fusion.3, f32[688,768]{1,0:T(8,128)S(1)} %fusion.11, bf16[4,688,1024]{2,1,0:T(8,128)(2,1)} %collective-permute-done.2, bf16[768,4096]{1,0:T(8,128)(2,1)} %all-gather.6.cloned.1.call-done, ...), kind=kOutput, calls=%fused_computation.1 | convolution fusion | flops 4339086336 | bytes 34697220 | tf_op jit(solution)/shard_map/td,qjd->qjt/dot_general | solution.py:30
  407.6 0.1 reduce_sum.18
  407.7 11.8 %psum.7 = f32[6,4]{0,1:T(4,128)S(1)} all-reduce(f32[6,4]{0,1:T(4,128)S(1)} %bitcast.25), channel_id=1, replica_groups=mesh['dp'=4,'tensor'=8] {'tensor'}, use_global_device_ids=true, to_apply=%region_2.3 | all-reduce | flops 24 | bytes 192 | tf_op jit(solution)/shard_map/psum | solution.py:43
  419.5 0.6 broadcast_multiply_fusion
  (1 shorter events, 0.0 us)
Async XLA Ops:
  6.5 52.0 %all-gather.4.cloned.1.call-start = ((), (), s32[]{:S(2)}) async-start(), calls=%async_computation | async-start | bytes 7077888 | tf_op jit(solution)/shard_map/all_gather | solution.py:8
  7.3 260.5 %all-gather.8.cloned.1.call-start = ((), (), s32[]{:S(2)}) async-start(), calls=%async_computation.2 | async-start | bytes 9510912 | tf_op jit(solution)/shard_map/all_gather | solution.py:15
  8.0 270.7 %all-gather.6.cloned.1.call-start = ((), (), s32[]{:S(2)}) async-start(), calls=%async_computation.1 | async-start | bytes 7077888 | tf_op jit(solution)/shard_map/all_gather | solution.py:10
  8.1 3.5 copy-start
  16.0 251.6 %copy-start.1 = (s32[6]{0:T(128)S(1)}, s32[6]{0:T(128)}, u32[]{:S(2)}) copy-start(s32[6]{0:T(128)} %param.15) | copy-start | bytes 76
  16.0 126.9 %collective-permute-start = (bf16[4,688,1024]{2,1,0:T(8,128)(2,1)}, bf16[4,688,1024]{2,1,0:T(8,128)(2,1)}, u32[]{:S(2)}, u32[]{:S(2)}) collective-permute-start(bf16[4,688,1024]{2,1,0:T(8,128)(2,1)} %divide_convert_fusion), channel_id=1, source_target_pairs={{0,8},{8,16},{16,24},{24,0},{1,9},{9,17},{17,25},{25,1},{2,10},{10... | collective-permute-start | bytes 16908296 | tf_op jit(solution)/shard_map/ppermute | solution.py:29
  142.9 124.7 %collective-permute-start.1 = (bf16[4,688,1024]{2,1,0:T(8,128)(2,1)}, bf16[4,688,1024]{2,1,0:T(8,128)(2,1)}, u32[]{:S(2)}, u32[]{:S(2)}) collective-permute-start(bf16[4,688,1024]{2,1,0:T(8,128)(2,1)} %collective-permute-done), channel_id=1, source_target_pairs={{0,8},{8,16},{16,24},{24,0},{1,9},{9,17},{17,25},{25,1},{2,10},{10... | collective-permute-start | bytes 16908296 | tf_op jit(solution)/shard_map/ppermute | solution.py:29
  267.6 123.9 %collective-permute-start.2 = (bf16[4,688,1024]{2,1,0:T(8,128)(2,1)}, bf16[4,688,1024]{2,1,0:T(8,128)(2,1)}, u32[]{:S(2)}, u32[]{:S(2)}) collective-permute-start(bf16[4,688,1024]{2,1,0:T(8,128)(2,1)} %collective-permute-done.1), channel_id=1, source_target_pairs={{0,8},{8,16},{16,24},{24,0},{1,9},{9,17},{17,25},{25,1},{2,10},{10... | collective-permute-start | bytes 16908296 | tf_op jit(solution)/shard_map/ppermute | solution.py:29
  278.7 11.1 %copy-start.2 = (bf16[768,4096]{1,0:T(8,128)(2,1)S(1)}, bf16[768,4096]{1,0:T(8,128)(2,1)}, u32[]{:S(2)}) copy-start(bf16[768,4096]{1,0:T(8,128)(2,1)} %all-gather.6.cloned.1.call-done) | copy-start | bytes 18874372
Sparse Core Ops, SparseCore 0:
  9.2 49.2 all-gather.3
  60.4 54.5 all-gather.7
  116.9 46.5 all-gather.5
